TPU v7x, 256 devices: a whole 4x4x8 slice. The times are simulated.
256 devices in a mesh: ops: 4 (over y), blk: 64 (over x, z, core).
Axes of the slice: x: 4, y: 4, z: 8, core: 2. Of those that a mesh axis runs over, the one named last changes fastest.
Arguments:
- psi: bfloat16 [16384, 8192], P('blk'), may hold values from -6 to 6
- left_env: bfloat16 [16, 64, 256, 256], P('ops', 'blk'), may hold values from -0.09375 to 0.09375
- right_env: bfloat16 [16, 64, 128, 128], P('ops', 'blk'), may hold values from -0.5 to 0.5
- left_live: int32 [64], replicated, may hold values from 64 to 256, as said below
- right_live: int32 [64], replicated, may hold values from 32 to 128, as said below
Outputs:
- hpsi: float32 [16384, 8192], P('blk', 'ops')
Inputs may be any that keep to these rules, and one draw needn't show every extreme that they name: `left_live`: some left sector is fully live. `right_live`: some right sector is fully live.
All inputs are finite; a program needn't handle non-finite values.
Results may differ from a plain program's by a relative error of at most 0.0029.
Values may be sent and summed in bfloat16 or wider, within the bound.
No kernel may reach another device: no remote copies, remote signals or barrier semaphores. Data moves between devices by JAX's collectives and lax.ppermute only.
A program may use at most 128 MiB of HBM per device.

v0:
```python
import jax
import jax.numpy as jnp
from jax import lax
from jax.sharding import PartitionSpec as P


def shards(psi, left_env, right_env, left_live, right_live):
    sectors = lax.axis_size("blk")
    rows = psi.shape[0]
    columns = psi.shape[1]
    width = columns // sectors
    mine = lax.axis_index("blk")
    row_live = lax.dynamic_index_in_dim(left_live, mine, keepdims=False)
    row_mask = jnp.arange(rows, dtype=jnp.int32) < row_live
    col_mask = (jnp.arange(width, dtype=jnp.int32)[None, :] < right_live[:, None]).reshape(columns)
    masked = jnp.where(row_mask[:, None] & col_mask[None, :], psi, jnp.zeros_like(psi))
    groups = lax.axis_size("ops")
    share = columns // groups
    share_start = lax.axis_index("ops") * share
    share_mask = lax.dynamic_slice_in_dim(col_mask, share_start, share)
    terms = left_env.shape[0]
    lefts = left_env[:, 0]
    rights = lax.all_gather(right_env, "blk", axis=1, tiled=True)
    partial_value = jnp.zeros((rows, sectors, width), jnp.float32)
    for t in range(terms):
        mixed = jnp.dot(lefts[t], masked, preferred_element_type=jnp.float32).astype(jnp.bfloat16)
        mixed = mixed.reshape(rows, sectors, width)
        partial_value = partial_value + jnp.einsum(
            "ajr,jsr->ajs", mixed, rights[t], preferred_element_type=jnp.float32
        )
    partial_value = partial_value.reshape(rows, columns)
    summed = lax.psum_scatter(partial_value, "ops", scatter_dimension=1, tiled=True)
    return jnp.where(row_mask[:, None] & share_mask[None, :], summed, jnp.zeros_like(summed))


def solution(mesh):
    in_specs = (P("blk", None), P("ops", "blk", None, None), P("ops", "blk", None, None), P(), P())
    out_specs = P("blk", "ops")
    return jax.shard_map(shards, mesh=mesh, in_specs=in_specs, out_specs=out_specs, check_vma=False)
```

profile of v0, /device:TPU:1, one launch (start us, length us, event | category | flops | bytes accessed | tf_op | source)
XLA Modules:
  0.0 224.4 jit_solution(11705806541663982912)
XLA Ops:
  6.5 0.0 all-gather.2.cloned.1.call-start
  6.5 0.7 all-gather.2.cloned.1.call-update
  7.3 0.0 reduce-scatter.2.cloned.1.call-start
  7.3 1.2 dynamic_slice.7
  8.5 0.6 iota_compare_fusion.1
  9.2 0.7 fusion.11
  9.9 0.0 copy-start.3
  10.0 0.0 copy-start.4
  10.0 6.2 %convolution_convert_fusion.2 = bf16[8192,256]{1,0:T(8,128)(2,1)} fusion(bf16[4,1,256,256]{3,2,1,0:T(8,128)(2,1)} %param.6, bf16[256,8192]{1,0:T(8,128)(2,1)} %param.5, pred[8192]{0:T(1024)(128)(4,1)S(1)} %fusion.11, pred[256]{0:T(512)(128)(4,1)S(1)} %iota_compare_fusion.1), kind=kOutput, calls=%fused_computation.2 | convolution fusion | flops 1080033280 | bytes 8528128 | tf_op jit(solution)/shard_map/dot_general | solution.py:26
  16.2 0.0 copy-done.3
  16.2 0.0 copy-done.4
  16.2 4.2 %convolution_convert_fusion.3 = bf16[8192,256]{1,0:T(8,128)(2,1)} fusion(bf16[4,1,256,256]{3,2,1,0:T(8,128)(2,1)S(1)} %copy-done.4, bf16[256,8192]{1,0:T(8,128)(2,1)S(1)} %copy-done.3, pred[8192]{0:T(1024)(128)(4,1)S(1)} %fusion.11, pred[256]{0:T(512)(128)(4,1)S(1)} %iota_compare_fusion.1), kind=kOutput, calls=%fused_computation.3 | convolution fusion | flops 1080033280 | bytes 8528384 | tf_op jit(solution)/shard_map/dot_general | solution.py:26
  20.3 4.1 %convolution_convert_fusion.1 = bf16[8192,256]{1,0:T(8,128)(2,1)} fusion(bf16[4,1,256,256]{3,2,1,0:T(8,128)(2,1)S(1)} %copy-done.4, bf16[256,8192]{1,0:T(8,128)(2,1)S(1)} %copy-done.3, pred[8192]{0:T(1024)(128)(4,1)S(1)} %fusion.11, pred[256]{0:T(512)(128)(4,1)S(1)} %iota_compare_fusion.1), kind=kOutput, calls=%fused_computation.1 | convolution fusion | flops 1080033280 | bytes 8528384 | tf_op jit(solution)/shard_map/dot_general | solution.py:26
  24.5 4.1 %convolution_convert_fusion = bf16[8192,256]{1,0:T(8,128)(2,1)} fusion(bf16[4,1,256,256]{3,2,1,0:T(8,128)(2,1)S(1)} %copy-done.4, bf16[256,8192]{1,0:T(8,128)(2,1)S(1)} %copy-done.3, pred[8192]{0:T(1024)(128)(4,1)S(1)} %fusion.11, pred[256]{0:T(512)(128)(4,1)S(1)} %iota_compare_fusion.1), kind=kOutput, calls=%fused_computation | convolution fusion | flops 1080033280 | bytes 8528384 | tf_op jit(solution)/shard_map/dot_general | solution.py:26
  28.6 68.6 %all-gather.2.cloned.1.call-done = bf16[4,64,128,128]{3,2,1,0:T(8,128)(2,1)} async-done(((bf16[4,1,128,128]{3,2,1,0:T(8,128)(2,1)}), bf16[4,64,128,128]{3,2,1,0:T(8,128)(2,1)}) %all-gather.2.cloned.1.call-update) | async-done | bytes 8388624 | tf_op jit(solution)/shard_map/all_gather | solution.py:23
  97.2 0.0 copy-start
  97.2 0.0 copy-start.2
  97.2 4.2 %fusion.1 = f32[64,256,128]{1,2,0:T(8,128)S(1)} fusion(bf16[256,64,128]{0,2,1:T(8,128)(2,1)} %bitcast.50, bf16[4,64,128,128]{3,2,1,0:T(8,128)(2,1)} %all-gather.2.cloned.1.call-done), kind=kOutput, calls=%fused_computation.10 | convolution fusion | flops 536870912 | bytes 14680064 | tf_op jit(solution)/shard_map/ajr,jsr->ajs/dot_general | solution.py:28
  101.5 1.0 copy-done
  102.5 1.2 copy-done.2
  103.7 0.0 copy-start.1
  103.7 4.5 %fusion.2 = f32[64,256,128]{1,2,0:T(8,128)} fusion(bf16[256,64,128]{0,2,1:T(8,128)(2,1)S(1)} %bitcast.49, bf16[4,64,128,128]{3,2,1,0:T(8,128)(2,1)S(1)} %copy-done), kind=kOutput, calls=%fused_computation.12 | convolution fusion | flops 536870912 | bytes 14680064 | tf_op jit(solution)/shard_map/ajr,jsr->ajs/dot_general | solution.py:28
  108.1 0.0 copy-done.1
  108.1 4.5 %fusion = f32[64,256,128]{1,2,0:T(8,128)} fusion(bf16[256,64,128]{0,2,1:T(8,128)(2,1)S(1)} %bitcast.48, bf16[4,64,128,128]{3,2,1,0:T(8,128)(2,1)S(1)} %copy-done), kind=kOutput, calls=%fused_computation.8 | convolution fusion | flops 536870912 | bytes 14680064 | tf_op jit(solution)/shard_map/ajr,jsr->ajs/dot_general | solution.py:28
  112.6 13.2 %add_add_fusion = f32[64,256,128]{1,2,0:T(8,128)} fusion(f32[64,256,128]{1,2,0:T(8,128)} %fusion, f32[64,256,128]{1,2,0:T(8,128)} %fusion.2, f32[64,256,128]{1,2,0:T(8,128)S(1)} %fusion.1, bf16[256,64,128]{0,2,1:T(8,128)(2,1)} %bitcast.47, bf16[4,64,128,128]{3,2,1,0:T(8,128)(2,1)} %all-gather.2.cloned.1.call-done), kind=kOutput, calls=%fused_computation.4 | convolution fusion | flops 543162368 | bytes 39845888 | tf_op jit(solution)/shard_map/ajr,jsr->ajs/dot_general | solution.py:28
  125.8 8.9 %copy.10 = f32[256,8192]{1,0:T(8,128)} copy(f32[256,8192]{0,1:T(8,128)} %bitcast.46) | data formatting | bytes 16777216 | tf_op jit(solution)/shard_map/reshape | solution.py:31
  134.7 0.0 reduce-scatter.2.cloned.1.call-update
  134.8 79.6 %reduce-scatter.2.cloned.1.call-done = f32[256,2048]{1,0:T(8,128)} async-done(((f32[256,8192]{1,0:T(8,128)}), f32[256,2048]{1,0:T(8,128)}) %reduce-scatter.2.cloned.1.call-update) | async-done | bytes 2097168 | tf_op jit(solution)/shard_map/reduce_scatter | solution.py:32
  214.4 3.2 %and_select_fusion.1 = f32[256,2048]{1,0:T(8,128)} fusion(f32[256,2048]{1,0:T(8,128)} %reduce-scatter.2.cloned.1.call-done, pred[2048]{0:T(1024)(128)(4,1)S(1)} %dynamic_slice.8, pred[256]{0:T(512)(128)(4,1)S(1)} %iota_compare_fusion.1), kind=kLoop, calls=%fused_computation.13 | loop fusion | flops 1048576 | bytes 4196608 | tf_op jit(solution)/shard_map/jit(_where)/select_n | solution.py:33
  (1 shorter events, 0.0 us)
Async XLA Ops:
  6.5 90.7 %all-gather.2.cloned.1.call-start = ((), (), s32[]{:S(2)}) async-start(), calls=%async_computation.1 | async-start | bytes 8519680 | tf_op jit(solution)/shard_map/all_gather | solution.py:23
  7.3 207.1 %reduce-scatter.2.cloned.1.call-start = ((), (), s32[]{:S(2)}) async-start(), calls=%async_computation.2 | async-start | bytes 10485760 | tf_op jit(solution)/shard_map/reduce_scatter | solution.py:32
  9.9 6.2 %copy-start.3 = (bf16[256,8192]{1,0:T(8,128)(2,1)S(1)}, bf16[256,8192]{1,0:T(8,128)(2,1)}, u32[]{:S(2)}) copy-start(bf16[256,8192]{1,0:T(8,128)(2,1)} %param.5) | copy-start | bytes 12582916
  10.0 6.2 %copy-start.4 = (bf16[4,1,256,256]{3,2,1,0:T(8,128)(2,1)S(1)}, bf16[4,1,256,256]{3,2,1,0:T(8,128)(2,1)}, u32[]{:S(2)}) copy-start(bf16[4,1,256,256]{3,2,1,0:T(8,128)(2,1)} %param.6) | copy-start | bytes 1572868
  97.2 5.2 %copy-start = (bf16[4,64,128,128]{3,2,1,0:T(8,128)(2,1)S(1)}, bf16[4,64,128,128]{3,2,1,0:T(8,128)(2,1)}, u32[]{:S(2)}) copy-start(bf16[4,64,128,128]{3,2,1,0:T(8,128)(2,1)} %all-gather.2.cloned.1.call-done) | copy-start | bytes 25165828
  97.2 6.4 %copy-start.2 = (bf16[8192,256]{1,0:T(8,128)(2,1)S(1)}, bf16[8192,256]{1,0:T(8,128)(2,1)}, u32[]{:S(2)}) copy-start(bf16[8192,256]{1,0:T(8,128)(2,1)} %convolution_convert_fusion.3) | copy-start | bytes 12582916
  103.7 4.5 %copy-start.1 = (bf16[8192,256]{1,0:T(8,128)(2,1)S(1)}, bf16[8192,256]{1,0:T(8,128)(2,1)}, u32[]{:S(2)}) copy-start(bf16[8192,256]{1,0:T(8,128)(2,1)} %convolution_convert_fusion.1) | copy-start | bytes 12582916
Sparse Core Ops, SparseCore 0:
  10.1 87.0 all-gather.1
  134.9 79.4 reduce-scatter.1
where the time goes:
time: 225 us; the launch traced here: 224 us
  waiting for transfers between devices  149 us (66%)
  matrix products  45 us (20%)
  between operations  13.5 us (6%)
  local copies, waits for them, and re-layouts  12.4 us (6%)
  other arithmetic  4.57 us (2%)
    reduce_scatter x1, waiting for transfers between devices, shards(): lax.psum_scatter(partial_value, 'ops', scatter_dimension=1, tiled=True)  79.6 us
    all_gather x1, waiting for transfers between devices, shards(): rights = lax.all_gather(right_env, 'blk', axis=1, tiled=True)  68.6 us
    dot_general x4, matrix products, shards(): jnp.einsum('ajr,jsr->ajs', mixed, rights[t], preferred_element_type=jnp.f...  26.4 us
    dot_general x4, matrix products, shards(): jnp.dot(lefts[t], masked, preferred_element_type=jnp.float32)  18.6 us
    reshape x1, local copies, waits for them, and re-layouts, shards(): partial_value = partial_value.reshape(rows, columns)  8.9 us
  transfers between devices with their start and end apart: 2, of which 2 were waited for; matrix products, arithmetic and copies ran while one was open for 9% of the time, Pallas kernels for 0%

commit v1 on v0

--- a/solution.py
+++ b/solution.py
@@ -20,7 +20,10 @@
     share_mask = lax.dynamic_slice_in_dim(col_mask, share_start, share)
     terms = left_env.shape[0]
     lefts = left_env[:, 0]
-    rights = lax.all_gather(right_env, "blk", axis=1, tiled=True)
+    resolve_the_record = lambda load, array_dim: jnp.concatenate(
+        jax.lax.all_to_all(jnp.stack([load] * jax.lax.axis_size("blk"), 0), "blk", 0, 0), array_dim
+    )
+    rights = resolve_the_record(right_env, 1)
     partial_value = jnp.zeros((rows, sectors, width), jnp.float32)
     for t in range(terms):
         mixed = jnp.dot(lefts[t], masked, preferred_element_type=jnp.float32).astype(jnp.bfloat16)

time: 225 us -> 350 us (1.56)
  waiting for transfers between devices: 149 us -> 245 us
  local copies, waits for them, and re-layouts: 12.4 us -> 28.3 us
  starting transfers between devices: 0.04 us -> 13.5 us
    all_to_all x0 -> x1, waiting for transfers between devices: none -> 166 us  [shards(): jax.lax.all_to_all(jnp.stack([load] * jax.lax.axis_size('blk'), 0), 'blk'...]
    all_gather x1 -> x0, waiting for transfers between devices: 68.6 us -> none  [shards(): rights = lax.all_gather(right_env, 'blk', axis=1, tiled=True)]
    all_to_all x0 -> x1, starting transfers between devices: none -> 13.3 us  [shards(): jax.lax.all_to_all(jnp.stack([load] * jax.lax.axis_size('blk'), 0), 'blk'...]
    all_to_all x0 -> x1, local copies, waits for them, and re-layouts: none -> 10.3 us  [shards(): jax.lax.all_to_all(jnp.stack([load] * jax.lax.axis_size('blk'), 0), 'blk'...]
    another operation x0 -> x1, local copies, waits for them, and re-layouts: none -> 6.26 us  [shards(): jnp.stack([load] * jax.lax.axis_size('blk'), 0)]
  transfers between devices with their start and end apart: 2 -> 2, of which waited for: 2 -> 2; matrix products, arithmetic and copies ran while one was open for 9% -> 6% of each run, Pallas kernels for 0% -> 0%
where the time goes in v1:
time: 350 us
  waiting for transfers between devices  245 us (70%)
  matrix products  45.2 us (13%)
  local copies, waits for them, and re-layouts  28.3 us (8%)
  starting transfers between devices  13.5 us (4%)
  between operations  13.5 us (4%)
  other arithmetic  3.92 us (1%)
    all_to_all x1, waiting for transfers between devices, shards(): jax.lax.all_to_all(jnp.stack([load] * jax.lax.axis_size('blk'), 0), 'blk'...  166 us
    reduce_scatter x1, waiting for transfers between devices, shards(): lax.psum_scatter(partial_value, 'ops', scatter_dimension=1, tiled=True)  79.8 us
    dot_general x4, matrix products, shards(): jnp.einsum('ajr,jsr->ajs', mixed, rights[t], preferred_element_type=jnp.f...  26.6 us
    dot_general x4, matrix products, shards(): jnp.dot(lefts[t], masked, preferred_element_type=jnp.float32)  18.6 us
    all_to_all x1, starting transfers between devices, shards(): jax.lax.all_to_all(jnp.stack([load] * jax.lax.axis_size('blk'), 0), 'blk'...  13.3 us
    all_to_all x1, local copies, waits for them, and re-layouts, shards(): jax.lax.all_to_all(jnp.stack([load] * jax.lax.axis_size('blk'), 0), 'blk'...  10.3 us
    reshape x1, local copies, waits for them, and re-layouts, shards(): partial_value = partial_value.reshape(rows, columns)  8.91 us
  transfers between devices with their start and end apart: 2, of which 2 were waited for; matrix products, arithmetic and copies ran while one was open for 6% of the time, Pallas kernels for 0%

profile of v1, /device:TPU:1, one launch (start us, length us, event | category | flops | bytes accessed | tf_op | source)
XLA Modules:
  0.0 349.8 jit_solution(13419207221584529534)
XLA Ops:
  6.5 6.3 %stack.2 = bf16[64,4,1,128,128]{4,3,2,1,0:T(8,128)(2,1)} broadcast(bf16[4,128,128]{2,1,0:T(8,128)(2,1)} %bitcast.59), dimensions={1,3,4} | broadcast | bytes 8519680 | tf_op jit(solution)/shard_map/stack | solution.py:24
  12.8 0.0 copy-start.6
  12.8 0.0 copy-start.3
  12.8 0.0 copy-start.5
  12.8 13.3 %all-to-all-start = ((bf16[64,4,1,128,128]{4,3,2,1,0:T(8,128)(2,1)}), bf16[64,4,1,128,128]{4,3,2,1,0:T(8,128)(2,1)}, u32[]{:S(2)}, u32[]{:S(2)}) async-start(bf16[64,4,1,128,128]{4,3,2,1,0:T(8,128)(2,1)} %stack.2), calls=%async_computation | async-start | bytes 16777216 | tf_op jit(solution)/shard_map/all_to_all | solution.py:24
  26.1 0.2 reduce-scatter.2.cloned.1.call-start
  26.3 0.0 copy-done.6
  26.3 0.6 dynamic_slice.7
  26.9 0.6 iota_compare_fusion.1
  27.6 0.0 copy-done.3
  27.6 0.1 fusion.11
  27.7 0.0 copy-done.5
  27.7 0.0 copy-start.4
  27.7 6.2 %convolution_convert_fusion.2 = bf16[8192,256]{1,0:T(8,128)(2,1)} fusion(bf16[4,1,256,256]{3,2,1,0:T(8,128)(2,1)S(1)} %copy-done.5, bf16[256,8192]{1,0:T(8,128)(2,1)} %param.5, pred[8192]{0:T(1024)(128)(4,1)S(1)} %fusion.11, pred[256]{0:T(512)(128)(4,1)S(1)} %iota_compare_fusion.1), kind=kOutput, calls=%fused_computation.2 | convolution fusion | flops 1080033280 | bytes 8528384 | tf_op jit(solution)/shard_map/dot_general | solution.py:29
  33.9 0.0 copy-done.4
  33.9 4.1 %convolution_convert_fusion.3 = bf16[8192,256]{1,0:T(8,128)(2,1)} fusion(bf16[4,1,256,256]{3,2,1,0:T(8,128)(2,1)S(1)} %copy-done.5, bf16[256,8192]{1,0:T(8,128)(2,1)S(1)} %copy-done.4, pred[8192]{0:T(1024)(128)(4,1)S(1)} %fusion.11, pred[256]{0:T(512)(128)(4,1)S(1)} %iota_compare_fusion.1), kind=kOutput, calls=%fused_computation.3 | convolution fusion | flops 1080033280 | bytes 8528384 | tf_op jit(solution)/shard_map/dot_general | solution.py:29
  38.0 4.1 %convolution_convert_fusion.1 = bf16[8192,256]{1,0:T(8,128)(2,1)} fusion(bf16[4,1,256,256]{3,2,1,0:T(8,128)(2,1)S(1)} %copy-done.5, bf16[256,8192]{1,0:T(8,128)(2,1)S(1)} %copy-done.4, pred[8192]{0:T(1024)(128)(4,1)S(1)} %fusion.11, pred[256]{0:T(512)(128)(4,1)S(1)} %iota_compare_fusion.1), kind=kOutput, calls=%fused_computation.1 | convolution fusion | flops 1080033280 | bytes 8528384 | tf_op jit(solution)/shard_map/dot_general | solution.py:29
  42.2 4.2 %convolution_convert_fusion = bf16[8192,256]{1,0:T(8,128)(2,1)} fusion(bf16[4,1,256,256]{3,2,1,0:T(8,128)(2,1)S(1)} %copy-done.5, bf16[256,8192]{1,0:T(8,128)(2,1)S(1)} %copy-done.4, pred[8192]{0:T(1024)(128)(4,1)S(1)} %fusion.11, pred[256]{0:T(512)(128)(4,1)S(1)} %iota_compare_fusion.1), kind=kOutput, calls=%fused_computation | convolution fusion | flops 1080033280 | bytes 8528384 | tf_op jit(solution)/shard_map/dot_general | solution.py:29
  46.3 165.5 %all-to-all-done = bf16[64,4,1,128,128]{4,3,2,1,0:T(8,128)(2,1)} async-done(((bf16[64,4,1,128,128]{4,3,2,1,0:T(8,128)(2,1)}), bf16[64,4,1,128,128]{4,3,2,1,0:T(8,128)(2,1)}, u32[]{:S(2)}, u32[]{:S(2)}) %all-to-all-start) | async-done | bytes 8388640 | tf_op jit(solution)/shard_map/all_to_all | solution.py:24
  211.8 10.3 %copy.22 = bf16[64,4,1,128,128]{4,3,0,2,1:T(8,128)(2,1)} copy(bf16[64,4,1,128,128]{4,3,2,1,0:T(8,128)(2,1)} %all-to-all-done) | data formatting | bytes 16777216 | tf_op jit(solution)/shard_map/all_to_all | solution.py:24
  222.2 0.0 copy-start
  222.2 0.0 copy-start.2
  222.2 4.2 %fusion.1 = f32[64,256,128]{1,2,0:T(8,128)S(1)} fusion(bf16[256,64,128]{0,2,1:T(8,128)(2,1)} %bitcast.58, bf16[4,64,1,128,128]{4,3,1,2,0:T(8,128)(2,1)} %bitcast.50), kind=kOutput, calls=%fused_computation.11 | convolution fusion | flops 536870912 | bytes 14680064 | tf_op jit(solution)/shard_map/ajr,jsr->ajs/dot_general | solution.py:31
  226.4 1.0 copy-done
  227.4 1.2 copy-done.2
  228.6 0.0 copy-start.1
  228.6 4.5 %fusion.2 = f32[64,256,128]{1,2,0:T(8,128)} fusion(bf16[256,64,128]{0,2,1:T(8,128)(2,1)S(1)} %bitcast.57, bf16[4,64,1,128,128]{4,3,1,2,0:T(8,128)(2,1)S(1)} %bitcast.52), kind=kOutput, calls=%fused_computation.13 | convolution fusion | flops 536870912 | bytes 14680064 | tf_op jit(solution)/shard_map/ajr,jsr->ajs/dot_general | solution.py:31
  233.1 0.0 copy-done.1
  233.1 4.7 %fusion = f32[64,256,128]{1,2,0:T(8,128)} fusion(bf16[256,64,128]{0,2,1:T(8,128)(2,1)S(1)} %bitcast.56, bf16[4,64,1,128,128]{4,3,1,2,0:T(8,128)(2,1)S(1)} %bitcast.53), kind=kOutput, calls=%fused_computation.9 | convolution fusion | flops 536870912 | bytes 14680064 | tf_op jit(solution)/shard_map/ajr,jsr->ajs/dot_general | solution.py:31
  237.8 13.2 %add_add_fusion = f32[64,256,128]{1,2,0:T(8,128)} fusion(f32[64,256,128]{1,2,0:T(8,128)} %fusion, f32[64,256,128]{1,2,0:T(8,128)} %fusion.2, f32[64,256,128]{1,2,0:T(8,128)S(1)} %fusion.1, bf16[256,64,128]{0,2,1:T(8,128)(2,1)} %bitcast.55, bf16[4,64,1,128,128]{4,3,1,2,0:T(8,128)(2,1)} %bitcast.51), kind=kOutput, calls=%fused_computation.5 | convolution fusion | flops 543162368 | bytes 39845888 | tf_op jit(solution)/shard_map/ajr,jsr->ajs/dot_general | solution.py:31
  251.0 8.9 %copy.16 = f32[256,8192]{1,0:T(8,128)} copy(f32[256,8192]{0,1:T(8,128)} %bitcast.54) | data formatting | bytes 16777216 | tf_op jit(solution)/shard_map/reshape | solution.py:34
  259.9 0.0 reduce-scatter.2.cloned.1.call-update
  260.0 79.8 %reduce-scatter.2.cloned.1.call-done = f32[256,2048]{1,0:T(8,128)} async-done(((f32[256,8192]{1,0:T(8,128)}), f32[256,2048]{1,0:T(8,128)}) %reduce-scatter.2.cloned.1.call-update) | async-done | bytes 2097168 | tf_op jit(solution)/shard_map/reduce_scatter | solution.py:35
  339.8 3.2 and_select_fusion.1
  (1 shorter events, 0.0 us)
Async XLA Ops:
  12.8 13.5 %copy-start.6 = (s32[64]{0:T(128)S(1)}, s32[64]{0:T(128)}, u32[]{:S(2)}) copy-start(s32[64]{0:T(128)} %param.8) | copy-start | bytes 772
  12.8 14.8 %copy-start.3 = (s32[64]{0:T(128)S(1)}, s32[64]{0:T(128)}, u32[]{:S(2)}) copy-start(s32[64]{0:T(128)} %param.9) | copy-start | bytes 772
  12.8 14.9 %copy-start.5 = (bf16[4,1,256,256]{3,2,1,0:T(8,128)(2,1)S(1)}, bf16[4,1,256,256]{3,2,1,0:T(8,128)(2,1)}, u32[]{:S(2)}) copy-start(bf16[4,1,256,256]{3,2,1,0:T(8,128)(2,1)} %param.6) | copy-start | bytes 1572868
  12.8 199.0 %all-to-all-start = ((bf16[64,4,1,128,128]{4,3,2,1,0:T(8,128)(2,1)}), bf16[64,4,1,128,128]{4,3,2,1,0:T(8,128)(2,1)}, u32[]{:S(2)}, u32[]{:S(2)}) async-start(bf16[64,4,1,128,128]{4,3,2,1,0:T(8,128)(2,1)} %stack.2), calls=%async_computation | async-start | bytes 16777216 | tf_op jit(solution)/shard_map/all_to_all | solution.py:24
  26.1 313.7 %reduce-scatter.2.cloned.1.call-start = ((), (), s32[]{:S(2)}) async-start(), calls=%async_computation.2 | async-start | bytes 10485760 | tf_op jit(solution)/shard_map/reduce_scatter | solution.py:35
  27.7 6.2 %copy-start.4 = (bf16[256,8192]{1,0:T(8,128)(2,1)S(1)}, bf16[256,8192]{1,0:T(8,128)(2,1)}, u32[]{:S(2)}) copy-start(bf16[256,8192]{1,0:T(8,128)(2,1)} %param.5) | copy-start | bytes 12582916
  222.2 5.2 %copy-start = (bf16[64,4,1,128,128]{4,3,0,2,1:T(8,128)(2,1)S(1)}, bf16[64,4,1,128,128]{4,3,0,2,1:T(8,128)(2,1)}, u32[]{:S(2)}) copy-start(bf16[64,4,1,128,128]{4,3,0,2,1:T(8,128)(2,1)} %copy.22) | copy-start | bytes 25165828
  222.2 6.4 %copy-start.2 = (bf16[8192,256]{1,0:T(8,128)(2,1)S(1)}, bf16[8192,256]{1,0:T(8,128)(2,1)}, u32[]{:S(2)}) copy-start(bf16[8192,256]{1,0:T(8,128)(2,1)} %convolution_convert_fusion.3) | copy-start | bytes 12582916
  228.6 4.5 %copy-start.1 = (bf16[8192,256]{1,0:T(8,128)(2,1)S(1)}, bf16[8192,256]{1,0:T(8,128)(2,1)}, u32[]{:S(2)}) copy-start(bf16[8192,256]{1,0:T(8,128)(2,1)} %convolution_convert_fusion.1) | copy-start | bytes 12582916
Sparse Core Ops, SparseCore 0:
  260.1 79.6 reduce-scatter.1
